TPU v7x, 128 devices: a whole 4x4x4 slice. The times are simulated.
128 devices in a mesh: chain: 8 (over x, core), tile: 16 (over z, y).
Axes of the slice: x: 4, y: 4, z: 4, core: 2. Of those that a mesh axis runs over, the one named last changes fastest.
Arguments:
- frames: bfloat16 [16, 64, 128, 384], P('chain', 'tile'), may hold values from -6 to 6
- live_rows: int32 [16], P('tile'), may hold values from 1 to 4, as said below
- gain_first: float32 [384], replicated, may hold values from 0.1 to 1.9
- conv_first: bfloat16 [3, 3, 3, 384, 384], replicated, may hold values from -0.078125 to 0.078125
- gain_second: float32 [384], replicated, may hold values from 0.1 to 1.9
- conv_second: bfloat16 [3, 3, 3, 384, 384], replicated, may hold values from -0.078125 to 0.078125
Outputs:
- decoded: bfloat16 [16, 64, 128, 384], P('chain', 'tile')
Inputs may be any that keep to these rules, and one draw needn't show every extreme that they name: `live_rows`: some tile has all 4 rows live.
All inputs are finite; a program needn't handle non-finite values.
Results may differ from a plain program's by a relative error of at most 0.0047.
Values may be sent and summed in bfloat16 or wider, within the bound.
A program may use at most 64 MiB of HBM per device.

v0:
```python
import jax
import jax.numpy as jnp
from jax import lax
from jax.sharding import PartitionSpec as P


def from_behind(block, axis, distance):
    devices = range(lax.axis_size(axis))
    route = [(i - distance, i) for i in devices if i - distance in devices]
    return lax.ppermute(block, axis, route)


def with_halo(cells, sides, width):
    for axis, dim in sides:
        count = lax.axis_size(axis)
        ends = count - 1
        head = lax.slice_in_dim(cells, 0, width, axis=dim)
        tail = lax.slice_in_dim(cells, cells.shape[dim] - width, cells.shape[dim], axis=dim)
        cells = jnp.concatenate(
            [
                lax.ppermute(tail, axis, [(i, (i + 1) % count) for i in range(ends)]),
                cells,
                lax.ppermute(head, axis, [((i + 1) % count, i) for i in range(ends)]),
            ],
            axis=dim,
        )
    return cells


def activate(value, gain):
    value = value.astype(jnp.float32)
    meansq = jnp.mean(value * value, axis=-1, keepdims=True)
    return jax.nn.silu(value * jax.lax.rsqrt(meansq + 1e-06) * gain)


def convolve(source, weights):
    nframe, nrow, ncol, width = source.shape
    earlier = from_behind(source, "chain", 1)
    extended = jnp.concatenate([earlier, source], axis=0)
    extended = with_halo(extended, (("tile", 1),), 1)
    extended = jnp.pad(extended, ((0, 0), (0, 0), (1, 1), (0, 0)))
    total = jnp.zeros((nframe * nrow * ncol, width), jnp.float32)
    for kt in range(3):
        for kh in range(3):
            window = extended[kt : kt + nframe, kh : kh + nrow]
            stacked = jnp.concatenate([window[:, :, kw : kw + ncol] for kw in range(3)], axis=-1)
            stacked = stacked.reshape(nframe * nrow * ncol, 3 * width)
            taps = weights[kt, kh].reshape(3 * width, width)
            total = total + jnp.dot(stacked, taps, preferred_element_type=jnp.float32)
    return total.reshape(nframe, nrow, ncol, width)


def shards(frames, live_rows, gain_first, conv_first, gain_second, conv_second):
    nrow = frames.shape[1]
    mask = (jnp.arange(nrow, dtype=jnp.int32) < live_rows[0]).astype(jnp.float32)[
        None, :, None, None
    ]
    first = (mask * activate(frames, gain_first)).astype(jnp.bfloat16)
    hidden = convolve(first, conv_first)
    second = (mask * activate(hidden, gain_second)).astype(jnp.bfloat16)
    out = convolve(second, conv_second)
    return (mask * (frames.astype(jnp.float32) + out)).astype(jnp.bfloat16)


def solution(mesh):
    placed = (P("chain", "tile", None, None), P("tile"), P(), P(), P(), P())
    return jax.shard_map(
        shards,
        mesh=mesh,
        in_specs=placed,
        out_specs=P("chain", "tile", None, None),
        check_vma=False,
    )
```

profile of v0, /device:TPU:26, one launch (start us, length us, event | category | flops | bytes accessed | tf_op | source)
XLA Modules:
  0.0 116.6 jit_solution(11403796338912061496)
XLA Ops:
  2.0 1.7 %fusion.23 = bf16[2,4,128,384]{3,2,1,0:T(8,128)(2,1)S(1)} fusion(bf16[2,4,128,384]{3,2,1,0:T(8,128)(2,1)} %param.6, f32[384]{0:T(512)} %param.8, f32[2,4,128]{2,1,0:T(4,128)S(1)} %add_rsqrt_fusion.1, f32[4]{0:T(128)S(1)} %compare_convert_fusion), kind=kLoop, calls=%fused_computation.52 | loop fusion | flops 3538944 | bytes 1578512 | tf_op jit(solution)/shard_map/convert_element_type | solution.py:58
  3.8 1.9 %collective-permute-start = (bf16[2,4,128,384]{3,2,1,0:T(8,128)(2,1)S(1)}, bf16[2,4,128,384]{3,2,1,0:T(8,128)(2,1)S(1)}, u32[]{:S(2)}, u32[]{:S(2)}) collective-permute-start(bf16[2,4,128,384]{3,2,1,0:T(8,128)(2,1)S(1)} %fusion.23), channel_id=1, source_target_pairs={{0,16},{16,32},{32,48},{48,64},{64,80},{80,96},{96,112},{1,17},{17... | collective-permute-start | bytes 2359304 | tf_op jit(solution)/shard_map/ppermute | solution.py:10
  5.7 11.4 %collective-permute-done = bf16[2,4,128,384]{3,2,1,0:T(8,128)(2,1)S(1)} collective-permute-done((bf16[2,4,128,384]{3,2,1,0:T(8,128)(2,1)S(1)}, bf16[2,4,128,384]{3,2,1,0:T(8,128)(2,1)S(1)}, u32[]{:S(2)}, u32[]{:S(2)}) %collective-permute-start) | collective-permute-done | bytes 786464 | tf_op jit(solution)/shard_map/ppermute | solution.py:10
  17.2 3.5 %collective-permute-start.1 = (bf16[4,1,128,384]{3,2,1,0:T(8,128)(2,1)S(1)}, bf16[4,1,128,384]{3,2,1,0:T(8,128)(2,1)S(1)}, u32[]{:S(2)}, u32[]{:S(2)}) collective-permute-start(bf16[4,1,128,384]{3,2,1,0:T(8,128)(2,1)S(1)} %get-tuple-element.77), channel_id=1, source_target_pairs={{0,1},{1,2},{2,3},{3,4},{4,5},{5,6},{6,7},{7,8},{8,9},{9,10},{10,1... | collective-permute-start | bytes 1179656 | tf_op jit(solution)/shard_map/ppermute | solution.py:21
  20.6 2.4 %collective-permute-start.2 = (bf16[4,1,128,384]{3,2,1,0:T(8,128)(2,1)S(1)}, bf16[4,1,128,384]{3,2,1,0:T(8,128)(2,1)S(1)}, u32[]{:S(2)}, u32[]{:S(2)}) collective-permute-start(bf16[4,1,128,384]{3,2,1,0:T(8,128)(2,1)S(1)} %get-tuple-element.78), channel_id=1, source_target_pairs={{1,0},{2,1},{3,2},{4,3},{5,4},{6,5},{7,6},{8,7},{9,8},{10,9},{11,1... | collective-permute-start | bytes 1179656 | tf_op jit(solution)/shard_map/ppermute | solution.py:23
  23.0 4.8 %fusion.27 = (bf16[1,1,3,384,384]{4,3,2,1,0:T(8,128)(2,1)S(1)}, bf16[1,1,3,384,384]{4,3,2,1,0:T(8,128)(2,1)S(1)}, bf16[1,1,3,384,384]{4,3,2,1,0:T(8,128)(2,1)S(1...) fusion(bf16[3,3,3,384,384]{4,3,2,1,0:T(8,128)(2,1)} %param.9), kind=kLoop, calls=%fused_computation.67 | loop fusion | bytes 15925248 | tf_op jit(solution)/shard_map/slice | solution.py:48
  29.2 5.3 %collective-permute-done.2 = bf16[4,1,128,384]{3,2,1,0:T(8,128)(2,1)S(1)} collective-permute-done((bf16[4,1,128,384]{3,2,1,0:T(8,128)(2,1)S(1)}, bf16[4,1,128,384]{3,2,1,0:T(8,128)(2,1)S(1)}, u32[]{:S(2)}, u32[]{:S(2)}) %collective-permute-start.2) | collective-permute-done | bytes 393248 | tf_op jit(solution)/shard_map/ppermute | solution.py:23
  34.5 1.7 %fusion.8 = bf16[4,6,130,384]{3,2,1,0:T(8,128)(2,1)S(1)} fusion(bf16[4,1,128,384]{3,2,1,0:T(8,128)(2,1)S(1)} %collective-permute-done.2, bf16[4,1,128,384]{3,2,1,0:T(8,128)(2,1)S(1)} %collective-permute-done.1, bf16[2,4,128,384]{3,2,1,0:T(8,128)(2,1)S(1)} %fusion.23, bf16[2,4,128,384]{3,2,1,0:T(8,128)(2,1)S(1)} %collective-permute-done), kind=kLoop, calls=%fused_computation.12 | loop fusion | flops 17971200 | bytes 4755456 | tf_op jit(solution)/shard_map/concatenate | solution.py:19
  36.3 3.4 %fusion.29 = (bf16[2,4,128,384]{3,2,1,0:T(8,128)(2,1)S(1)}, bf16[2,4,128,384]{3,2,1,0:T(8,128)(2,1)S(1)}, bf16[2,4,128,384]{3,2,1,0:T(8,128)(2,1)S(1)}, bf16[2,4...) fusion(bf16[4,6,130,384]{3,2,1,0:T(8,128)(2,1)S(1)} %fusion.8), kind=kLoop, calls=%fused_computation.69 | loop fusion | bytes 28311552 | tf_op jit(solution)/shard_map/slice | solution.py:46
  50.5 1.4 %fusion.38 = f32[1024,384]{1,0:T(8,128)S(1)} fusion(bf16[1024,1152]{1,0:T(8,128)(2,1)S(1)} %bitcast.87, bf16[1152,384]{1,0:T(8,128)(2,1)S(1)} %bitcast.107), kind=kOutput, calls=%fused_computation.78 | convolution fusion | flops 905969664 | bytes 4816896 | tf_op jit(solution)/shard_map/dot_general | solution.py:49
  52.2 1.4 %fusion.39 = f32[1024,384]{1,0:T(8,128)S(1)} fusion(bf16[1024,1152]{1,0:T(8,128)(2,1)S(1)} %bitcast.94, bf16[1152,384]{1,0:T(8,128)(2,1)S(1)} %bitcast.106), kind=kOutput, calls=%fused_computation.79 | convolution fusion | flops 905969664 | bytes 4816896 | tf_op jit(solution)/shard_map/dot_general | solution.py:49
  55.4 1.4 %fusion.41 = f32[1024,384]{1,0:T(8,128)S(1)} fusion(bf16[1024,1152]{1,0:T(8,128)(2,1)S(1)} %bitcast.85, bf16[1152,384]{1,0:T(8,128)(2,1)S(1)} %bitcast.102), kind=kOutput, calls=%fused_computation.81 | convolution fusion | flops 905969664 | bytes 4816896 | tf_op jit(solution)/shard_map/dot_general | solution.py:49
  57.2 2.0 %multiply_reduce_fusion = (f32[1024]{0:T(1024)S(1)}, f32[1024,384]{1,0:T(8,128)S(1)}) fusion(bf16[1024,1152]{1,0:T(8,128)(2,1)S(1)} %bitcast.77, bf16[1152,384]{1,0:T(8,128)(2,1)S(1)} %bitcast.83, f32[1024,384]{1,0:T(8,128)S(1)} %fusion.41, f32[1024,384]{1,0:T(8,128)S(1)} %fusion.40, f32[1024,384]{1,0:T(8,128)S(1)} %fusion.39, f32[1024,384]{1,0:T(8,128)S(1)} %fusion.38, ...), kind=kOutput, calls=%fused_computation.57 | convolution fusion | flops 909900800 | bytes 17403904 | tf_op jit(solution)/shard_map/dot_general | solution.py:49
  59.8 1.9 %collective-permute-start.3 = (bf16[2,4,128,384]{3,2,1,0:T(8,128)(2,1)S(1)}, bf16[2,4,128,384]{3,2,1,0:T(8,128)(2,1)S(1)}, u32[]{:S(2)}, u32[]{:S(2)}) collective-permute-start(bf16[2,4,128,384]{3,2,1,0:T(8,128)(2,1)S(1)} %multiply_convert_fusion), channel_id=1, source_target_pairs={{0,16},{16,32},{32,48},{48,64},{64,80},{80,96},{96,112},{1,17},{17... | collective-permute-start | bytes 2359304 | tf_op jit(solution)/shard_map/ppermute | solution.py:10
  61.7 11.4 %collective-permute-done.3 = bf16[2,4,128,384]{3,2,1,0:T(8,128)(2,1)S(1)} collective-permute-done((bf16[2,4,128,384]{3,2,1,0:T(8,128)(2,1)S(1)}, bf16[2,4,128,384]{3,2,1,0:T(8,128)(2,1)S(1)}, u32[]{:S(2)}, u32[]{:S(2)}) %collective-permute-start.3) | collective-permute-done | bytes 786464 | tf_op jit(solution)/shard_map/ppermute | solution.py:10
  73.2 1.9 %collective-permute-start.4 = (bf16[4,1,128,384]{3,2,1,0:T(8,128)(2,1)S(1)}, bf16[4,1,128,384]{3,2,1,0:T(8,128)(2,1)S(1)}, u32[]{:S(2)}, u32[]{:S(2)}) collective-permute-start(bf16[4,1,128,384]{3,2,1,0:T(8,128)(2,1)S(1)} %get-tuple-element.73), channel_id=1, source_target_pairs={{0,1},{1,2},{2,3},{3,4},{4,5},{5,6},{6,7},{7,8},{8,9},{9,10},{10,1... | collective-permute-start | bytes 1179656 | tf_op jit(solution)/shard_map/ppermute | solution.py:21
  75.1 3.9 %collective-permute-start.5 = (bf16[4,1,128,384]{3,2,1,0:T(8,128)(2,1)S(1)}, bf16[4,1,128,384]{3,2,1,0:T(8,128)(2,1)S(1)}, u32[]{:S(2)}, u32[]{:S(2)}) collective-permute-start(bf16[4,1,128,384]{3,2,1,0:T(8,128)(2,1)S(1)} %get-tuple-element.74), channel_id=1, source_target_pairs={{1,0},{2,1},{3,2},{4,3},{5,4},{6,5},{7,6},{8,7},{9,8},{10,9},{11,1... | collective-permute-start | bytes 1179656 | tf_op jit(solution)/shard_map/ppermute | solution.py:23
  79.1 3.1 %fusion.26 = (bf16[1,1,3,384,384]{4,3,2,1,0:T(8,128)(2,1)S(1)}, bf16[1,1,3,384,384]{4,3,2,1,0:T(8,128)(2,1)}, bf16[1,1,3,384,384]{4,3,2,1,0:T(8,128)(2,1)}, bf16...) fusion(bf16[3,3,3,384,384]{4,3,2,1,0:T(8,128)(2,1)S(1)} %bitcast.80), kind=kLoop, calls=%fused_computation.66 | loop fusion | bytes 15925248 | tf_op jit(solution)/shard_map/slice | solution.py:48
  82.2 2.7 %collective-permute-done.4 = bf16[4,1,128,384]{3,2,1,0:T(8,128)(2,1)S(1)} collective-permute-done((bf16[4,1,128,384]{3,2,1,0:T(8,128)(2,1)S(1)}, bf16[4,1,128,384]{3,2,1,0:T(8,128)(2,1)S(1)}, u32[]{:S(2)}, u32[]{:S(2)}) %collective-permute-start.4) | collective-permute-done | bytes 393248 | tf_op jit(solution)/shard_map/ppermute | solution.py:21
  84.9 4.0 %collective-permute-done.5 = bf16[4,1,128,384]{3,2,1,0:T(8,128)(2,1)S(1)} collective-permute-done((bf16[4,1,128,384]{3,2,1,0:T(8,128)(2,1)S(1)}, bf16[4,1,128,384]{3,2,1,0:T(8,128)(2,1)S(1)}, u32[]{:S(2)}, u32[]{:S(2)}) %collective-permute-start.5) | collective-permute-done | bytes 393248 | tf_op jit(solution)/shard_map/ppermute | solution.py:23
  89.9 1.8 %select_maximum_fusion = bf16[4,6,130,384]{3,2,1,0:T(8,128)(2,1)S(1)} fusion(bf16[4,1,128,384]{3,2,1,0:T(8,128)(2,1)S(1)} %collective-permute-done.5, bf16[4,1,128,384]{3,2,1,0:T(8,128)(2,1)S(1)} %collective-permute-done.4, bf16[2,4,128,384]{3,2,1,0:T(8,128)(2,1)S(1)} %multiply_convert_fusion, bf16[2,4,128,384]{3,2,1,0:T(8,128)(2,1)S(1)} %collective-permute-done.3), kind=kLoop, calls=%fused_computation.3 | loop fusion | flops 17971200 | bytes 4755456 | tf_op jit(solution)/shard_map/concatenate | solution.py:19
  91.7 3.4 %fusion.28 = (bf16[2,4,128,384]{3,2,1,0:T(8,128)(2,1)S(1)}, bf16[2,4,128,384]{3,2,1,0:T(8,128)(2,1)S(1)}, bf16[2,4,128,384]{3,2,1,0:T(8,128)(2,1)S(1)}, bf16[2,4...) fusion(bf16[4,6,130,384]{3,2,1,0:T(8,128)(2,1)S(1)} %select_max, ...), kind=kLoop, calls=%fused_computation.68 | loop fusion | bytes 28311552 | tf_op jit(solution)/shard_map/slice | solution.py:46
  111.9 1.4 %fusion.49 = f32[1024,384]{1,0:T(8,128)S(1)} fusion(bf16[1024,1152]{1,0:T(8,128)(2,1)S(1)} %bitcast.86, bf16[1152,384]{1,0:T(8,128)(2,1)S(1)} %bitcast.101), kind=kOutput, calls=%fused_computation.89 | convolution fusion | flops 905969664 | bytes 4816896 | tf_op jit(solution)/shard_map/dot_general | solution.py:49
  113.6 1.7 %add_add_fusion = f32[1024,384]{1,0:T(8,128)S(1)} fusion(f32[1024,384]{1,0:T(8,128)S(1)} %fusion.49, f32[1024,384]{1,0:T(8,128)S(1)} %fusion.48, f32[1024,384]{1,0:T(8,128)S(1)} %fusion.47, f32[1024,384]{1,0:T(8,128)S(1)} %fusion.46, f32[1024,384]{1,0:T(8,128)S(1)} %fusion.45, f32[1024,384]{1,0:T(8,128)S(1)} %fusion.44, f32[1024,384]{1,0:T(8,128)S(1)} %fusion.42, ...), kind=kOutput, calls=%fused_computation.55 | convolution fusion | flops 909115392 | bytes 17399808 | tf_op jit(solution)/shard_map/dot_general | solution.py:49
  (65 shorter events, 35.6 us)
Async XLA Ops:
  3.8 13.3 %collective-permute-start = (bf16[2,4,128,384]{3,2,1,0:T(8,128)(2,1)S(1)}, bf16[2,4,128,384]{3,2,1,0:T(8,128)(2,1)S(1)}, u32[]{:S(2)}, u32[]{:S(2)}) collective-permute-start(bf16[2,4,128,384]{3,2,1,0:T(8,128)(2,1)S(1)} %fusion.23), channel_id=1, source_target_pairs={{0,16},{16,32},{32,48},{48,64},{64,80},{80,96},{96,112},{1,17},{17... | collective-permute-start | bytes 2359304 | tf_op jit(solution)/shard_map/ppermute | solution.py:10
  17.2 12.0 %collective-permute-start.1 = (bf16[4,1,128,384]{3,2,1,0:T(8,128)(2,1)S(1)}, bf16[4,1,128,384]{3,2,1,0:T(8,128)(2,1)S(1)}, u32[]{:S(2)}, u32[]{:S(2)}) collective-permute-start(bf16[4,1,128,384]{3,2,1,0:T(8,128)(2,1)S(1)} %get-tuple-element.77), channel_id=1, source_target_pairs={{0,1},{1,2},{2,3},{3,4},{4,5},{5,6},{6,7},{7,8},{8,9},{9,10},{10,1... | collective-permute-start | bytes 1179656 | tf_op jit(solution)/shard_map/ppermute | solution.py:21
  20.6 13.9 %collective-permute-start.2 = (bf16[4,1,128,384]{3,2,1,0:T(8,128)(2,1)S(1)}, bf16[4,1,128,384]{3,2,1,0:T(8,128)(2,1)S(1)}, u32[]{:S(2)}, u32[]{:S(2)}) collective-permute-start(bf16[4,1,128,384]{3,2,1,0:T(8,128)(2,1)S(1)} %get-tuple-element.78), channel_id=1, source_target_pairs={{1,0},{2,1},{3,2},{4,3},{5,4},{6,5},{7,6},{8,7},{9,8},{10,9},{11,1... | collective-permute-start | bytes 1179656 | tf_op jit(solution)/shard_map/ppermute | solution.py:23
  41.0 1.2 %copy-start.8 = (bf16[1,1,3,384,384]{4,3,2,1,0:T(8,128)(2,1)S(1)}, bf16[1,1,3,384,384]{4,3,2,1,0:T(8,128)(2,1)}, u32[]{:S(2)}) copy-start(bf16[1,1,3,384,384]{4,3,2,1,0:T(8,128)(2,1)} %get-tuple-element.21) | copy-start | bytes 2654212
  45.4 1.2 %copy-start.6 = (bf16[1,1,3,384,384]{4,3,2,1,0:T(8,128)(2,1)S(1)}, bf16[1,1,3,384,384]{4,3,2,1,0:T(8,128)(2,1)}, u32[]{:S(2)}) copy-start(bf16[1,1,3,384,384]{4,3,2,1,0:T(8,128)(2,1)} %get-tuple-element.18) | copy-start | bytes 2654212
  57.2 21.9 %slice-start = ((s8[7962624]{0:T(1024)(128)(4,1)}), s8[4194304]{0:T(1024)(128)(4,1)S(1)}, s32[]{:S(2)}) async-start(s8[7962624]{0:T(1024)(128)(4,1)} %bitcast.79), calls=%async_computation | async-start | bytes 8388608
  57.2 2.0 %copy-start.9 = (f32[384]{0:T(512)S(1)}, f32[384]{0:T(512)}, u32[]{:S(2)}) copy-start(f32[384]{0:T(512)} %param.10) | copy-start | bytes 4612
  57.2 21.8 %slice-start.1 = ((s8[7962624]{0:T(1024)(128)(4,1)}), s8[3768320]{0:T(1024)(128)(4,1)S(1)}, s32[]{:S(2)}) async-start(s8[7962624]{0:T(1024)(128)(4,1)} %bitcast.79), calls=%async_computation.1 | async-start | bytes 7536640
  59.8 13.3 %collective-permute-start.3 = (bf16[2,4,128,384]{3,2,1,0:T(8,128)(2,1)S(1)}, bf16[2,4,128,384]{3,2,1,0:T(8,128)(2,1)S(1)}, u32[]{:S(2)}, u32[]{:S(2)}) collective-permute-start(bf16[2,4,128,384]{3,2,1,0:T(8,128)(2,1)S(1)} %multiply_convert_fusion), channel_id=1, source_target_pairs={{0,16},{16,32},{32,48},{48,64},{64,80},{80,96},{96,112},{1,17},{17... | collective-permute-start | bytes 2359304 | tf_op jit(solution)/shard_map/ppermute | solution.py:10
  73.2 11.8 %collective-permute-start.4 = (bf16[4,1,128,384]{3,2,1,0:T(8,128)(2,1)S(1)}, bf16[4,1,128,384]{3,2,1,0:T(8,128)(2,1)S(1)}, u32[]{:S(2)}, u32[]{:S(2)}) collective-permute-start(bf16[4,1,128,384]{3,2,1,0:T(8,128)(2,1)S(1)} %get-tuple-element.73), channel_id=1, source_target_pairs={{0,1},{1,2},{2,3},{3,4},{4,5},{5,6},{6,7},{7,8},{8,9},{9,10},{10,1... | collective-permute-start | bytes 1179656 | tf_op jit(solution)/shard_map/ppermute | solution.py:21
  75.1 13.9 %collective-permute-start.5 = (bf16[4,1,128,384]{3,2,1,0:T(8,128)(2,1)S(1)}, bf16[4,1,128,384]{3,2,1,0:T(8,128)(2,1)S(1)}, u32[]{:S(2)}, u32[]{:S(2)}) collective-permute-start(bf16[4,1,128,384]{3,2,1,0:T(8,128)(2,1)S(1)} %get-tuple-element.74), channel_id=1, source_target_pairs={{1,0},{2,1},{3,2},{4,3},{5,4},{6,5},{7,6},{8,7},{9,8},{10,9},{11,1... | collective-permute-start | bytes 1179656 | tf_op jit(solution)/shard_map/ppermute | solution.py:23
  95.4 1.2 %copy-start.7 = (bf16[1,1,3,384,384]{4,3,2,1,0:T(8,128)(2,1)S(1)}, bf16[1,1,3,384,384]{4,3,2,1,0:T(8,128)(2,1)}, u32[]{:S(2)}) copy-start(bf16[1,1,3,384,384]{4,3,2,1,0:T(8,128)(2,1)} %get-tuple-element.12) | copy-start | bytes 2654212
  99.8 1.2 %copy-start.5 = (bf16[1,1,3,384,384]{4,3,2,1,0:T(8,128)(2,1)S(1)}, bf16[1,1,3,384,384]{4,3,2,1,0:T(8,128)(2,1)}, u32[]{:S(2)}) copy-start(bf16[1,1,3,384,384]{4,3,2,1,0:T(8,128)(2,1)} %get-tuple-element.9) | copy-start | bytes 2654212
  102.4 1.2 %copy-start.4 = (bf16[1,1,3,384,384]{4,3,2,1,0:T(8,128)(2,1)S(1)}, bf16[1,1,3,384,384]{4,3,2,1,0:T(8,128)(2,1)}, u32[]{:S(2)}) copy-start(bf16[1,1,3,384,384]{4,3,2,1,0:T(8,128)(2,1)} %get-tuple-element.7) | copy-start | bytes 2654212
  105.0 1.2 %copy-start.3 = (bf16[1,1,3,384,384]{4,3,2,1,0:T(8,128)(2,1)S(1)}, bf16[1,1,3,384,384]{4,3,2,1,0:T(8,128)(2,1)}, u32[]{:S(2)}) copy-start(bf16[1,1,3,384,384]{4,3,2,1,0:T(8,128)(2,1)} %get-tuple-element.6) | copy-start | bytes 2654212
  107.6 1.4 %copy-start.2 = (bf16[1,1,3,384,384]{4,3,2,1,0:T(8,128)(2,1)S(1)}, bf16[1,1,3,384,384]{4,3,2,1,0:T(8,128)(2,1)}, u32[]{:S(2)}) copy-start(bf16[1,1,3,384,384]{4,3,2,1,0:T(8,128)(2,1)} %get-tuple-element.11) | copy-start | bytes 2654212
  109.0 1.5 %copy-start.1 = (bf16[1,1,3,384,384]{4,3,2,1,0:T(8,128)(2,1)S(1)}, bf16[1,1,3,384,384]{4,3,2,1,0:T(8,128)(2,1)}, u32[]{:S(2)}) copy-start(bf16[1,1,3,384,384]{4,3,2,1,0:T(8,128)(2,1)} %get-tuple-element.8) | copy-start | bytes 2654212
  113.6 1.8 %copy-start = (bf16[2,4,128,384]{3,2,1,0:T(8,128)(2,1)S(1)}, bf16[2,4,128,384]{3,2,1,0:T(8,128)(2,1)}, u32[]{:S(2)}) copy-start(bf16[2,4,128,384]{3,2,1,0:T(8,128)(2,1)} %param.6) | copy-start | bytes 2359300
where the time goes:
time: 117 us
  waiting for transfers between devices  36.2 us (31%)
  matrix products  26.7 us (23%)
  local copies, waits for them, and re-layouts  21.3 us (18%)
  other arithmetic  15.6 us (13%)
  starting transfers between devices  15.5 us (13%)
  between operations  1.22 us (1%)
    dot_general x18, matrix products, convolve(): total = total + jnp.dot(stacked, taps, preferred_element_type=jnp.float32)  26.7 us
    ppermute x2, waiting for transfers between devices, from_behind(): return lax.ppermute(block, axis, route)  22.8 us
    ppermute x2, waiting for transfers between devices, with_halo(): lax.ppermute(head, axis, [((i + 1) % count, i) for i in range(ends)])  9.36 us
    slice x5, local copies, waits for them, and re-layouts, convolve(): window[:, :, kw:kw + ncol]  8.2 us
    slice x2, local copies, waits for them, and re-layouts, convolve(): taps = weights[kt, kh].reshape(3 * width, width)  7.95 us
    ppermute x2, starting transfers between devices, with_halo(): lax.ppermute(head, axis, [((i + 1) % count, i) for i in range(ends)])  6.28 us
    concatenate x14, other arithmetic, convolve(): jnp.concatenate([window[:, :, kw:kw + ncol] for kw in range(3)], axis=-1)  5.92 us
    ppermute x2, starting transfers between devices, with_halo(): lax.ppermute(tail, axis, [(i, (i + 1) % count) for i in range(ends)])  5.41 us
  transfers between devices with their start and end apart: 6, of which 6 were waited for; matrix products, arithmetic and copies ran while one was open for 7% of the time, Pallas kernels for 0%

commit v1 on v0

v1 whole, which is shorter than its diff:
```python
import jax
import jax.numpy as jnp
from jax import lax
from jax.experimental import pallas as pl
from jax.experimental.pallas import tpu as pltpu
from jax.sharding import PartitionSpec as P

MESH = pl.DeviceIdType.MESH


def activate(value, gain, mask):
    meansq = jnp.mean(value * value, axis=-1, keepdims=True)
    half = value * lax.rsqrt(meansq + 1e-06) * (0.5 * gain)
    return (mask * (half + half * jnp.tanh(half))).astype(jnp.bfloat16)


def block_kernel(
    n_chain, n_tile,
    live, frames_hbm, gain1, gain2, conv1_hbm, conv2_hbm, out_hbm,
    frames, a1, a2, w1, w2, part, result,
    in_sem, w_sem, out_sem, send_sem, recv_sem,
):
    c = lax.axis_index("chain")
    t = lax.axis_index("tile")
    nframe, nrow, ncol, width = frames.shape
    taps = 3 * width

    load = pltpu.make_async_copy(frames_hbm, frames, in_sem)
    load.start()
    weight_copies = {}
    for k, (hbm, w) in enumerate(((conv1_hbm, w1), (conv2_hbm, w2))):
        for kt in (2, 1, 0):
            group = []
            for kh in range(3):
                for kw in range(3):
                    group.append(
                        pltpu.make_async_copy(
                            hbm.at[kt, kh, kw],
                            w.at[pl.ds((kt * 3 + kh) * width, width), pl.ds(kw * width, width)],
                            w_sem.at[k, kt, kh, kw],
                        )
                    )
            weight_copies[k, kt] = group
            for copy in group:
                copy.start()

    def need_weights(k, kt):
        for copy in weight_copies[k, kt]:
            copy.wait()

    barrier = pltpu.get_barrier_semaphore()
    for axis, index, count in (("chain", c, n_chain), ("tile", t, n_tile)):
        for step in (1, count - 1):
            pl.semaphore_signal(
                barrier, inc=1, device_id={axis: lax.rem(index + step, count)}, device_id_type=MESH
            )

    even = lax.rem(c, 2) == 0
    after = c > 0
    before = c < n_chain - 1
    above = t > 0
    below = t < n_tile - 1

    for a in (a1, a2):
        @pl.when(c == 0)
        def _():
            a[0:nframe] = jnp.zeros((nframe,) + a.shape[1:], a.dtype)

        @pl.when(t == 0)
        def _():
            for g in range(2 * nframe):
                a[g, 0] = jnp.zeros((ncol, width), a.dtype)

        @pl.when(t == n_tile - 1)
        def _():
            for g in range(2 * nframe):
                a[g, nrow + 1] = jnp.zeros((ncol, width), a.dtype)

    last = nrow + 1

    def route(k, f, kind):
        a = (a1, a2)[k]
        own, old = nframe + f, f
        up, down, onward = {"tile": t - 1}, {"tile": t + 1}, {"chain": c + 1}
        src, src_rows, dst, dst_rows, to, s, r = {
            "x_top": (own, (1, 1), old, (1, 1), onward, 0, 0),
            "x_bottom": (own, (nrow, 1), old, (nrow, 1), onward, 1, 1),
            "x_middle": (own, (2, nrow - 2), old, (2, nrow - 2), onward, 2, 2),
            "y_up": (own, (1, 1), own, (last, 1), up, 3, 3),
            "y_down": (own, (nrow, 1), own, (0, 1), down, 4, 4),
            "c_bottom": (own, (last, 1), old, (last, 1), onward, 5, 5),
            "c_top": (own, (0, 1), old, (0, 1), onward, 6, 6),
            "f_up": (old, (1, 1), old, (last, 1), up, 7, 5),
            "f_down": (old, (nrow, 1), old, (0, 1), down, 8, 6),
        }[kind]
        return pltpu.make_async_remote_copy(
            src_ref=a.at[src, pl.ds(*src_rows)],
            dst_ref=a.at[dst, pl.ds(*dst_rows)],
            send_sem=send_sem.at[k, f, s],
            recv_sem=recv_sem.at[k, f, r],
            device_id=to,
            device_id_type=MESH,
        )

    may_send = {
        "x_top": before, "x_bottom": before, "x_middle": before,
        "y_up": above, "y_down": below,
        "c_bottom": even & below, "c_top": even & above,
        "f_up": even & after & above, "f_down": even & after & below,
    }
    may_hear = {
        "x_top": after, "x_bottom": after, "x_middle": after,
        "y_up": below, "y_down": above,
        "c_bottom": after & below, "c_top": after & above,
    }

    def send(k, f, *kinds):
        for kind in kinds:
            @pl.when(may_send[kind])
            def _():
                route(k, f, kind).start()

    def hear(k, f, *kinds):
        for kind in kinds:
            @pl.when(may_hear[kind])
            def _():
                route(k, f, kind).wait_recv()

    def mask(row):
        return jnp.where(live[0] > row, 1.0, 0.0).astype(jnp.float32)

    def columns(g, rows, a):
        return [jnp.concatenate([a[g, r + kh] for r in rows], axis=0) for kh in range(3)]

    def accumulate(a, w, f, rows, kts, fresh):
        lhs = jnp.concatenate([piece for kt in kts for piece in columns(f + kt, rows, a)], axis=1)
        rhs = w[kts[0] * taps : (kts[-1] + 1) * taps]
        got = jnp.dot(lhs, rhs, preferred_element_type=jnp.float32)
        for at, r in enumerate(rows):
            piece = got[at * ncol : (at + 1) * ncol]
            part[f, r] = piece if fresh else part[f, r] + piece

    col = lax.broadcasted_iota(jnp.int32, (ncol, width), 0)

    def total(f, r):
        left = pltpu.roll(part[f, r, :, 0:width], 1, 0)
        right = pltpu.roll(part[f, r, :, 2 * width : 3 * width], ncol - 1, 0)
        return (
            jnp.where(col == 0, 0.0, left)
            + part[f, r, :, width : 2 * width]
            + jnp.where(col == ncol - 1, 0.0, right)
        )

    load.wait()
    for f in (0, 1):
        for r in (0, 3):
            a1[nframe + f, 1 + r] = activate(frames[f, r].astype(jnp.float32), gain1[...], mask(r))
    pl.semaphore_wait(barrier, 4)
    send(0, 0, "y_up", "y_down")
    send(0, 1, "x_top", "x_bottom", "y_up", "y_down")
    for r in (1, 2):
        a1[nframe + 1, 1 + r] = activate(frames[1, r].astype(jnp.float32), gain1[...], mask(r))
    send(0, 1, "x_middle")
    for r in (1, 2):
        a1[nframe, 1 + r] = activate(frames[0, r].astype(jnp.float32), gain1[...], mask(r))
    send(0, 0, "x_top", "x_bottom", "x_middle")

    inner, outer, every = (1, 2), (0, 3), (0, 1, 2, 3)

    need_weights(0, 2)
    accumulate(a1, w1, 0, inner, (2,), True)
    need_weights(0, 1)
    accumulate(a1, w1, 1, inner, (1, 2), True)
    hear(0, 0, "y_up", "y_down")
    send(0, 0, "c_top", "c_bottom")
    accumulate(a1, w1, 0, outer, (2,), True)
    hear(0, 1, "x_top", "x_bottom")
    send(0, 1, "f_up", "f_down")
    hear(0, 1, "y_up", "y_down")
    send(0, 1, "c_top", "c_bottom")
    accumulate(a1, w1, 1, outer, (1, 2), True)
    hear(0, 1, "x_middle", "c_top", "c_bottom")
    need_weights(0, 0)
    accumulate(a1, w1, 1, every, (0,), False)
    hear(0, 0, "x_top", "x_bottom")
    send(0, 0, "f_up", "f_down")
    for r in outer + inner:
        a2[nframe + 1, 1 + r] = activate(total(1, r), gain2[...], mask(r))
    send(1, 1, "x_top", "x_bottom", "y_up", "y_down", "x_middle")
    hear(0, 0, "x_middle", "c_top", "c_bottom")
    accumulate(a1, w1, 0, every, (0, 1), False)
    for r in outer + inner:
        a2[nframe, 1 + r] = activate(total(0, r), gain2[...], mask(r))
    send(1, 0, "y_up", "y_down", "x_top", "x_bottom", "x_middle")

    hear(1, 1, "y_up", "y_down")
    send(1, 1, "c_top", "c_bottom")
    hear(1, 1, "x_top", "x_bottom")
    send(1, 1, "f_up", "f_down")
    need_weights(1, 2)
    accumulate(a2, w2, 0, inner, (2,), True)
    need_weights(1, 1)
    accumulate(a2, w2, 1, inner, (1, 2), True)
    hear(1, 0, "y_up", "y_down")
    send(1, 0, "c_top", "c_bottom")
    accumulate(a2, w2, 0, outer, (2,), True)
    hear(1, 0, "x_top", "x_bottom")
    send(1, 0, "f_up", "f_down")
    accumulate(a2, w2, 1, outer, (1, 2), True)
    need_weights(1, 0)
    hear(1, 1, "x_middle", "c_top", "c_bottom")
    accumulate(a2, w2, 1, every, (0,), False)

    def finish(f):
        for r in every:
            value = frames[f, r].astype(jnp.float32) + total(f, r)
            result[f, r] = (mask(r) * value).astype(jnp.bfloat16)
        return pltpu.make_async_copy(result.at[f], out_hbm.at[f], out_sem.at[f])

    store1 = finish(1)
    store1.start()
    hear(1, 0, "x_middle", "c_top", "c_bottom")
    accumulate(a2, w2, 0, every, (0, 1), False)
    store0 = finish(0)
    store0.start()

    for k in (0, 1):
        for f in (0, 1):
            for kind in may_send:
                @pl.when(may_send[kind])
                def _():
                    route(k, f, kind).wait_send()
    store1.wait()
    store0.wait()


def shards(frames, live_rows, gain_first, conv_first, gain_second, conv_second):
    nframe, nrow, ncol, width = frames.shape
    halo = (2 * nframe, nrow + 2, ncol, width)
    taps = 9 * width
    vmem, hbm = pltpu.VMEM, pl.ANY
    n_chain, n_tile = lax.axis_size("chain"), lax.axis_size("tile")

    def kernel(*refs):
        block_kernel(n_chain, n_tile, *refs)

    return pl.pallas_call(
        kernel,
        out_shape=jax.ShapeDtypeStruct(frames.shape, frames.dtype),
        in_specs=[
            pl.BlockSpec(memory_space=pltpu.SMEM),
            pl.BlockSpec(memory_space=hbm),
            pl.BlockSpec(memory_space=vmem),
            pl.BlockSpec(memory_space=vmem),
            pl.BlockSpec(memory_space=hbm),
            pl.BlockSpec(memory_space=hbm),
        ],
        out_specs=pl.BlockSpec(memory_space=hbm),
        scratch_shapes=[
            vmem(frames.shape, jnp.bfloat16),
            vmem(halo, jnp.bfloat16),
            vmem(halo, jnp.bfloat16),
            vmem((taps, 3 * width), jnp.bfloat16),
            vmem((taps, 3 * width), jnp.bfloat16),
            vmem((nframe, nrow, ncol, 3 * width), jnp.float32),
            vmem(frames.shape, jnp.bfloat16),
            pltpu.SemaphoreType.DMA,
            pltpu.SemaphoreType.DMA((2, 3, 3, 3)),
            pltpu.SemaphoreType.DMA((2,)),
            pltpu.SemaphoreType.DMA((2, 2, 9)),
            pltpu.SemaphoreType.DMA((2, 2, 7)),
        ],
        compiler_params=pltpu.CompilerParams(
            collective_id=0, has_side_effects=True, vmem_limit_bytes=56 << 20
        ),
    )(
        live_rows,
        frames,
        gain_first.reshape(1, width),
        gain_second.reshape(1, width),
        conv_first,
        conv_second,
    )


def solution(mesh):
    placed = (P("chain", "tile", None, None), P("tile"), P(), P(), P(), P())
    return jax.shard_map(
        shards,
        mesh=mesh,
        in_specs=placed,
        out_specs=P("chain", "tile", None, None),
        check_vma=False,
    )
```

time: 117 us -> 52.5 us (0.45)
  the two profiles are of different devices: /device:TPU:26 before, /device:TPU:100 now
where the time goes in v1:
time: 52.5 us; the launch traced here: 52.3 us
  Pallas kernels  47 us (90%)
  local copies, waits for them, and re-layouts  4.59 us (9%)
  between operations  0.66 us (1%)
    pallas_call x1, Pallas kernels, shards(): pl.pallas_call(kernel, out_shape=jax.ShapeDtypeStruct(frames.shape, frame...  47 us
    unnamed x1, local copies, waits for them, and re-layouts  2.09 us
    reshape x1, local copies, waits for them, and re-layouts, shards(): gain_second.reshape(1, width)  1.26 us
    reshape x1, local copies, waits for them, and re-layouts, shards(): gain_first.reshape(1, width)  1.25 us

profile of v1, /device:TPU:100, one launch (start us, length us, event | category | flops | bytes accessed | tf_op | source)
XLA Modules:
  0.0 52.3 jit_solution(17077013341010974566)
XLA Ops:
  0.7 1.2 %reshape.6.refs_2_ = f32[1,384]{1,0:T(1,128)} reshape(f32[384]{0:T(512)} %param.8) | data formatting | bytes 3072 | tf_op jit(solution)/shard_map/reshape | solution.py:279
  1.9 1.3 %reshape.7.refs_3_ = f32[1,384]{1,0:T(1,128)} reshape(f32[384]{0:T(512)} %param.10) | data formatting | bytes 3072 | tf_op jit(solution)/shard_map/reshape | solution.py:280
  3.2 47.0 %shard_map.64 = bf16[2,4,128,384]{3,2,1,0:T(8,128)(2,1)} custom-call(s32[1]{0:T(128)S(6)} %copy.8.refs_0_, bf16[2,4,128,384]{3,2,1,0:T(8,128)(2,1)} %refs_1_.1, f32[1,384]{1,0:T(1,128)} %reshape.6.refs_2_, f32[1,384]{1,0:T(1,128)} %reshape.7.refs_3_, bf16[3,3,3,384,384]{4,3,2,1,0:T(8,128)(2,1)} %refs_4_.1, bf16[3,3,3,384,384]{4,3,2,1,0:T(8,128)(2,1)} %refs_5_.1), custom_call_target="tpu_custom_call" | custom-call | tf_op jit(solution)/shard_map/pallas_call | solution.py:247
  50.2 2.1 %copy.9 = bf16[2,4,128,384]{3,2,1,0:T(8,128)(2,1)} copy(bf16[2,4,128,384]{3,2,1,0:T(8,128)(2,1)} %shard_map.64) | data formatting | bytes 1572864

commit v2 on v1

v2 whole, which is shorter than its diff:
```python
import jax
import jax.numpy as jnp
from jax import lax
from jax.experimental import pallas as pl
from jax.experimental.pallas import tpu as pltpu
from jax.sharding import PartitionSpec as P

MESH = pl.DeviceIdType.MESH


def activate(value, gain, mask):
    meansq = jnp.mean(value * value, axis=-1, keepdims=True)
    half = value * lax.rsqrt(meansq + 1e-06) * (0.5 * gain).reshape(1, -1)
    return (mask * (half + half * jnp.tanh(half))).astype(jnp.bfloat16)


def block_kernel(
    n_chain, n_tile,
    live, frames_hbm, gain1_hbm, gain2_hbm, conv1_hbm, conv2_hbm, result,
    frames, gain1, gain2, a1, a2, w1, w2, part,
    in_sem, w_sem, send_sem, recv_sem,
):
    c = lax.axis_index("chain")
    t = lax.axis_index("tile")
    nframe, nrow, ncol, width = frames.shape
    taps = 3 * width

    loads = [
        pltpu.make_async_copy(src, dst, in_sem.at[i])
        for i, (src, dst) in enumerate(
            ((frames_hbm, frames), (gain1_hbm, gain1), (gain2_hbm, gain2))
        )
    ]
    for load in loads:
        load.start()
    weight_copies = {}
    for k, (hbm, w) in enumerate(((conv1_hbm, w1), (conv2_hbm, w2))):
        for kt in (2, 1, 0):
            group = []
            for kh in range(3):
                for kw in range(3):
                    group.append(
                        pltpu.make_async_copy(
                            hbm.at[kt, kh, kw],
                            w.at[pl.ds(kh * width, width), pl.ds((kt * 3 + kw) * width, width)],
                            w_sem.at[k, kt, kh, kw],
                        )
                    )
            weight_copies[k, kt] = group

    def fetch_weights(k, kt):
        for copy in weight_copies[k, kt]:
            copy.start()

    fetch_weights(0, 2)
    fetch_weights(0, 1)

    def need_weights(k, kt):
        for copy in weight_copies[k, kt]:
            copy.wait()

    barrier = pltpu.get_barrier_semaphore()
    for axis, index, count in (("chain", c, n_chain), ("tile", t, n_tile)):
        for step in (1, count - 1):
            pl.semaphore_signal(
                barrier, inc=1, device_id={axis: lax.rem(index + step, count)}, device_id_type=MESH
            )

    even = lax.rem(c, 2) == 0
    after = c > 0
    before = c < n_chain - 1
    above = t > 0
    below = t < n_tile - 1

    for a in (a1, a2):
        @pl.when(c == 0)
        def _():
            a[0:nframe] = jnp.zeros((nframe,) + a.shape[1:], a.dtype)

        @pl.when(t == 0)
        def _():
            for g in range(2 * nframe):
                a[g, 0] = jnp.zeros((ncol, width), a.dtype)

        @pl.when(t == n_tile - 1)
        def _():
            for g in range(2 * nframe):
                a[g, nrow + 1] = jnp.zeros((ncol, width), a.dtype)

    last = nrow + 1

    def route(k, f, kind):
        a = (a1, a2)[k]
        own, old = nframe + f, f
        up, down, onward = {"tile": t - 1}, {"tile": t + 1}, {"chain": c + 1}
        src, src_rows, dst, dst_rows, to, s, r = {
            "x_top": (own, (1, 1), old, (1, 1), onward, 0, 0),
            "x_bottom": (own, (nrow, 1), old, (nrow, 1), onward, 1, 1),
            "x_middle": (own, (2, nrow - 2), old, (2, nrow - 2), onward, 2, 2),
            "y_up": (own, (1, 1), own, (last, 1), up, 3, 3),
            "y_down": (own, (nrow, 1), own, (0, 1), down, 4, 4),
            "c_bottom": (own, (last, 1), old, (last, 1), onward, 5, 5),
            "c_top": (own, (0, 1), old, (0, 1), onward, 6, 6),
            "f_up": (old, (1, 1), old, (last, 1), up, 7, 5),
            "f_down": (old, (nrow, 1), old, (0, 1), down, 8, 6),
        }[kind]
        return pltpu.make_async_remote_copy(
            src_ref=a.at[src, pl.ds(*src_rows)],
            dst_ref=a.at[dst, pl.ds(*dst_rows)],
            send_sem=send_sem.at[k, f, s],
            recv_sem=recv_sem.at[k, f, r],
            device_id=to,
            device_id_type=MESH,
        )

    may_send = {
        "x_top": before, "x_bottom": before, "x_middle": before,
        "y_up": above, "y_down": below,
        "c_bottom": even & below, "c_top": even & above,
        "f_up": even & after & above, "f_down": even & after & below,
    }
    may_hear = {
        "x_top": after, "x_bottom": after, "x_middle": after,
        "y_up": below, "y_down": above,
        "c_bottom": after & below, "c_top": after & above,
    }

    def send(k, f, *kinds):
        for kind in kinds:
            @pl.when(may_send[kind])
            def _():
                route(k, f, kind).start()

    def hear(k, f, *kinds):
        for kind in kinds:
            @pl.when(may_hear[kind])
            def _():
                route(k, f, kind).wait_recv()

    def mask(row):
        return jnp.where(live[0] > row, 1.0, 0.0).astype(jnp.float32)

    def accumulate(a, w, g, rows):
        lhs = jnp.concatenate(
            [jnp.concatenate([a[g, r + kh] for r in rows], axis=0) for kh in range(3)], axis=1
        )
        kts = [kt for kt in range(3) if 0 <= g - kt < nframe]
        rhs = w[:, kts[0] * taps : (kts[-1] + 1) * taps]
        got = jnp.dot(lhs, rhs, preferred_element_type=jnp.float32)
        for n, kt in enumerate(kts):
            f = g - kt
            fresh = g == nframe + f
            for at, r in enumerate(rows):
                piece = got[at * ncol : (at + 1) * ncol, n * taps : (n + 1) * taps]
                part[f, r] = piece if fresh else part[f, r] + piece

    col = lax.broadcasted_iota(jnp.int32, (ncol, width), 0)

    def total(f, r):
        left = pltpu.roll(part[f, r, :, 0:width], 1, 0)
        right = pltpu.roll(part[f, r, :, 2 * width : 3 * width], ncol - 1, 0)
        return (
            jnp.where(col == 0, 0.0, left)
            + part[f, r, :, width : 2 * width]
            + jnp.where(col == ncol - 1, 0.0, right)
        )

    inner, outer = (1, 2), (0, 3)
    edges, halos, sides = ("x_top", "x_bottom"), ("c_top", "c_bottom"), ("y_up", "y_down")
    forwards = ("f_up", "f_down")

    def first(f, rows):
        for r in rows:
            a1[nframe + f, 1 + r] = activate(frames[f, r].astype(jnp.float32), gain1[...], mask(r))

    def second(f, rows):
        for r in rows:
            a2[nframe + f, 1 + r] = activate(total(f, r), gain2[...], mask(r))

    def decoded(f, rows):
        for r in rows:
            value = frames[f, r].astype(jnp.float32) + total(f, r)
            result[f, r] = (mask(r) * value).astype(jnp.bfloat16)

    for load in loads:
        load.wait()
    first(1, outer)
    pl.semaphore_wait(barrier, 4)
    send(0, 1, *sides, *edges)
    first(1, inner)
    first(0, outer)
    first(0, inner)
    fetch_weights(0, 0)

    need_weights(0, 2)
    accumulate(a1, w1, 3, inner)
    send(0, 1, "x_middle")
    send(0, 0, *sides)
    need_weights(0, 1)
    accumulate(a1, w1, 2, inner)
    send(0, 0, *edges, "x_middle")
    hear(0, 1, *sides)
    send(0, 1, *halos)
    hear(0, 1, *edges)
    send(0, 1, *forwards)
    fetch_weights(1, 2)
    accumulate(a1, w1, 3, outer)
    hear(0, 0, *sides)
    send(0, 0, *halos)
    accumulate(a1, w1, 2, outer)
    hear(0, 1, "x_middle")
    need_weights(0, 0)
    fetch_weights(1, 1)
    accumulate(a1, w1, 1, inner)
    hear(0, 0, *edges)
    send(0, 0, *forwards)
    second(1, inner)
    send(1, 1, "x_middle")
    hear(0, 1, *halos)
    fetch_weights(1, 0)
    accumulate(a1, w1, 1, outer)
    second(1, outer)
    send(1, 1, *sides, *edges)
    hear(0, 0, "x_middle")
    accumulate(a1, w1, 0, inner)
    second(0, inner)
    send(1, 0, "x_middle")
    hear(0, 0, *halos)
    accumulate(a1, w1, 0, outer)
    second(0, outer)
    send(1, 0, *sides, *edges)

    need_weights(1, 2)
    accumulate(a2, w2, 3, inner)
    hear(1, 1, *sides)
    send(1, 1, *halos)
    hear(1, 1, *edges)
    send(1, 1, *forwards)
    need_weights(1, 1)
    accumulate(a2, w2, 2, inner)
    accumulate(a2, w2, 3, outer)
    hear(1, 0, *sides)
    send(1, 0, *halos)
    hear(1, 0, *edges)
    send(1, 0, *forwards)
    accumulate(a2, w2, 2, outer)
    hear(1, 1, "x_middle")
    need_weights(1, 0)
    accumulate(a2, w2, 1, inner)
    hear(1, 1, *halos)
    decoded(1, inner)
    accumulate(a2, w2, 1, outer)
    hear(1, 0, "x_middle")
    decoded(1, outer)
    accumulate(a2, w2, 0, inner)
    hear(1, 0, *halos)
    decoded(0, inner)
    accumulate(a2, w2, 0, outer)
    decoded(0, outer)

    for k in (0, 1):
        for f in (0, 1):
            for kind in may_send:
                @pl.when(may_send[kind])
                def _():
                    route(k, f, kind).wait_send()


def shards(frames, live_rows, gain_first, conv_first, gain_second, conv_second):
    nframe, nrow, ncol, width = frames.shape
    halo = (2 * nframe, nrow + 2, ncol, width)
    taps = 3 * width
    vmem, hbm = pltpu.VMEM, pltpu.HBM
    n_chain, n_tile = lax.axis_size("chain"), lax.axis_size("tile")

    def kernel(*refs):
        block_kernel(n_chain, n_tile, *refs)

    return pl.pallas_call(
        kernel,
        out_shape=jax.ShapeDtypeStruct(frames.shape, frames.dtype),
        in_specs=[
            pl.BlockSpec(memory_space=pltpu.SMEM),
            pl.BlockSpec(memory_space=hbm),
            pl.BlockSpec(memory_space=hbm),
            pl.BlockSpec(memory_space=hbm),
            pl.BlockSpec(memory_space=hbm),
            pl.BlockSpec(memory_space=hbm),
        ],
        out_specs=pl.BlockSpec(memory_space=vmem),
        scratch_shapes=[
            vmem(frames.shape, jnp.bfloat16),
            vmem((width,), jnp.float32),
            vmem((width,), jnp.float32),
            vmem(halo, jnp.bfloat16),
            vmem(halo, jnp.bfloat16),
            vmem((taps, 3 * taps), jnp.bfloat16),
            vmem((taps, 3 * taps), jnp.bfloat16),
            vmem((nframe, nrow, ncol, taps), jnp.float32),
            pltpu.SemaphoreType.DMA((3,)),
            pltpu.SemaphoreType.DMA((2, 3, 3, 3)),
            pltpu.SemaphoreType.DMA((2, 2, 9)),
            pltpu.SemaphoreType.DMA((2, 2, 7)),
        ],
        compiler_params=pltpu.CompilerParams(
            collective_id=0, has_side_effects=True, vmem_limit_bytes=55750000
        ),
    )(
        live_rows,
        frames,
        gain_first,
        gain_second,
        conv_first,
        conv_second,
    )


def solution(mesh):
    placed = (P("chain", "tile", None, None), P("tile"), P(), P(), P(), P())
    return jax.shard_map(
        shards,
        mesh=mesh,
        in_specs=placed,
        out_specs=P("chain", "tile", None, None),
        check_vma=False,
    )
```

time: 52.5 us -> 37.6 us (0.72)
  the two profiles are of different devices: /device:TPU:100 before, /device:TPU:6 now
where the time goes in v2:
time: 37.6 us; the launch traced here: 37 us
  Pallas kernels  34.1 us (91%)
  local copies, waits for them, and re-layouts  2.24 us (6%)
  between operations  0.67 us (2%)
    pallas_call x1, Pallas kernels, shards(): pl.pallas_call(kernel, out_shape=jax.ShapeDtypeStruct(frames.shape, frame...  34.1 us
    unnamed x5, local copies, waits for them, and re-layouts  2.24 us

profile of v2, /device:TPU:6, one launch (start us, length us, event | category | flops | bytes accessed | tf_op | source)
XLA Modules:
  0.0 37.0 jit_solution(7220296122972166356)
XLA Ops:
  0.7 0.0 copy-start
  0.7 0.7 %copy-done = f32[384]{0:T(512)S(1)} copy-done((f32[384]{0:T(512)S(1)}, f32[384]{0:T(512)}, u32[]{:S(2)}) %copy-start) | copy-done | bytes 1560
  1.3 0.0 copy-start.1
  1.3 0.7 %copy-done.1 = f32[384]{0:T(512)S(1)} copy-done((f32[384]{0:T(512)S(1)}, f32[384]{0:T(512)}, u32[]{:S(2)}) %copy-start.1) | copy-done | bytes 1560
  2.0 34.1 %shard_map.64 = bf16[2,4,128,384]{3,2,1,0:T(8,128)(2,1)S(1)} custom-call(s32[1]{0:T(128)S(6)} %copy.8.refs_0_, bf16[2,4,128,384]{3,2,1,0:T(8,128)(2,1)} %refs_1_.1, f32[384]{0:T(512)S(1)} %copy-done, f32[384]{0:T(512)S(1)} %copy-done.1, bf16[3,3,3,384,384]{4,3,2,1,0:T(8,128)(2,1)} %refs_4_.1, bf16[3,3,3,384,384]{4,3,2,1,0:T(8,128)(2,1)} %refs_5_.1), custom_call_target="tpu_custom_call" | custom-call | tf_op jit(solution)/shard_map/pallas_call | solution.py:279
  36.1 0.9 %copy.9 = bf16[2,4,128,384]{3,2,1,0:T(8,128)(2,1)} copy(bf16[2,4,128,384]{3,2,1,0:T(8,128)(2,1)S(1)} %shard_map.64) | data formatting | bytes 1572864
Async XLA Ops:
  0.7 0.7 %copy-start = (f32[384]{0:T(512)S(1)}, f32[384]{0:T(512)}, u32[]{:S(2)}) copy-start(f32[384]{0:T(512)} %refs_2_.1) | copy-start | bytes 4612
  1.3 0.7 %copy-start.1 = (f32[384]{0:T(512)S(1)}, f32[384]{0:T(512)}, u32[]{:S(2)}) copy-start(f32[384]{0:T(512)} %refs_3_.1) | copy-start | bytes 4612

commit v3 on v2

--- a/solution.py
+++ b/solution.py
@@ -25,6 +25,13 @@
     nframe, nrow, ncol, width = frames.shape
     taps = 3 * width
 
+    barrier = pltpu.get_barrier_semaphore()
+    for axis, index, count in (("chain", c, n_chain), ("tile", t, n_tile)):
+        for step in (1, count - 1):
+            pl.semaphore_signal(
+                barrier, inc=1, device_id={axis: lax.rem(index + step, count)}, device_id_type=MESH
+            )
+
     loads = [
         pltpu.make_async_copy(src, dst, in_sem.at[i])
         for i, (src, dst) in enumerate(
@@ -33,20 +40,18 @@
     ]
     for load in loads:
         load.start()
-    weight_copies = {}
-    for k, (hbm, w) in enumerate(((conv1_hbm, w1), (conv2_hbm, w2))):
-        for kt in (2, 1, 0):
-            group = []
-            for kh in range(3):
-                for kw in range(3):
-                    group.append(
-                        pltpu.make_async_copy(
-                            hbm.at[kt, kh, kw],
-                            w.at[pl.ds(kh * width, width), pl.ds((kt * 3 + kw) * width, width)],
-                            w_sem.at[k, kt, kh, kw],
-                        )
-                    )
-            weight_copies[k, kt] = group
+    weight_copies = {
+        (k, kt): [
+            pltpu.make_async_copy(
+                hbm.at[kt, :, kw],
+                w.at[:, :, pl.ds((kt * 3 + kw) * width, width)],
+                w_sem.at[k, kt, kw],
+            )
+            for kw in range(3)
+        ]
+        for k, (hbm, w) in enumerate(((conv1_hbm, w1), (conv2_hbm, w2)))
+        for kt in range(3)
+    }
 
     def fetch_weights(k, kt):
         for copy in weight_copies[k, kt]:
@@ -58,13 +63,6 @@
     def need_weights(k, kt):
         for copy in weight_copies[k, kt]:
             copy.wait()
-
-    barrier = pltpu.get_barrier_semaphore()
-    for axis, index, count in (("chain", c, n_chain), ("tile", t, n_tile)):
-        for step in (1, count - 1):
-            pl.semaphore_signal(
-                barrier, inc=1, device_id={axis: lax.rem(index + step, count)}, device_id_type=MESH
-            )
 
     even = lax.rem(c, 2) == 0
     after = c > 0
@@ -140,19 +138,33 @@
     def mask(row):
         return jnp.where(live[0] > row, 1.0, 0.0).astype(jnp.float32)
 
+    begun, started = set(), set()
+
     def accumulate(a, w, g, rows):
         lhs = jnp.concatenate(
             [jnp.concatenate([a[g, r + kh] for r in rows], axis=0) for kh in range(3)], axis=1
         )
         kts = [kt for kt in range(3) if 0 <= g - kt < nframe]
-        rhs = w[:, kts[0] * taps : (kts[-1] + 1) * taps]
+        rhs = w[:, :, kts[0] * taps : (kts[-1] + 1) * taps].reshape(taps, len(kts) * taps)
         got = jnp.dot(lhs, rhs, preferred_element_type=jnp.float32)
         for n, kt in enumerate(kts):
             f = g - kt
-            fresh = g == nframe + f
+            fresh = (a is a2, f, rows) not in begun
+            begun.add((a is a2, f, rows))
             for at, r in enumerate(rows):
                 piece = got[at * ncol : (at + 1) * ncol, n * taps : (n + 1) * taps]
                 part[f, r] = piece if fresh else part[f, r] + piece
+
+    def partly(a, w, g, row, khs):
+        lhs = jnp.concatenate([a[g, row + kh] for kh in khs], axis=1)
+        kts = [kt for kt in range(3) if 0 <= g - kt < nframe]
+        rhs = w[khs[0] : khs[-1] + 1, :, kts[0] * taps : (kts[-1] + 1) * taps].reshape(len(khs) * width, len(kts) * taps)
+        got = jnp.dot(lhs, rhs, preferred_element_type=jnp.float32)
+        for n, kt in enumerate(kts):
+            f = g - kt
+            piece = got[:, n * taps : (n + 1) * taps]
+            part[f, row] = piece if (f, row) not in started else part[f, row] + piece
+            started.add((f, row))
 
     col = lax.broadcasted_iota(jnp.int32, (ncol, width), 0)
 
@@ -184,30 +196,38 @@
 
     for load in loads:
         load.wait()
+    first(0, outer)
     first(1, outer)
     pl.semaphore_wait(barrier, 4)
-    send(0, 1, *sides, *edges)
+    send(0, 0, *sides)
+    send(0, 1, *edges)
     first(1, inner)
-    first(0, outer)
     first(0, inner)
     fetch_weights(0, 0)
 
     need_weights(0, 2)
     accumulate(a1, w1, 3, inner)
-    send(0, 1, "x_middle")
-    send(0, 0, *sides)
+    send(0, 1, *sides, "x_middle")
     need_weights(0, 1)
     accumulate(a1, w1, 2, inner)
-    send(0, 0, *edges, "x_middle")
-    hear(0, 1, *sides)
-    send(0, 1, *halos)
+    send(0, 0, *edges)
+    partly(a1, w1, 2, 0, (1, 2))
+    partly(a1, w1, 2, 3, (0, 1))
+    send(0, 0, "x_middle")
+    partly(a1, w1, 3, 0, (1, 2))
+    partly(a1, w1, 3, 3, (0, 1))
+    hear(0, 0, *sides)
+    send(0, 0, *halos)
     hear(0, 1, *edges)
     send(0, 1, *forwards)
     fetch_weights(1, 2)
-    accumulate(a1, w1, 3, outer)
-    hear(0, 0, *sides)
-    send(0, 0, *halos)
-    accumulate(a1, w1, 2, outer)
+    partly(a1, w1, 2, 0, (0,))
+    partly(a1, w1, 2, 3, (2,))
+    hear(0, 1, *sides)
+    send(0, 1, *halos)
+    partly(a1, w1, 3, 0, (0,))
+    partly(a1, w1, 3, 3, (2,))
+    begun.update({(False, 0, outer), (False, 1, outer)})
     hear(0, 1, "x_middle")
     need_weights(0, 0)
     fetch_weights(1, 1)
@@ -215,23 +235,38 @@
     hear(0, 0, *edges)
     send(0, 0, *forwards)
     second(1, inner)
-    send(1, 1, "x_middle")
     hear(0, 1, *halos)
     fetch_weights(1, 0)
     accumulate(a1, w1, 1, outer)
     second(1, outer)
     send(1, 1, *sides, *edges)
     hear(0, 0, "x_middle")
-    accumulate(a1, w1, 0, inner)
-    second(0, inner)
-    send(1, 0, "x_middle")
-    hear(0, 0, *halos)
-    accumulate(a1, w1, 0, outer)
-    second(0, outer)
-    send(1, 0, *sides, *edges)
-
     need_weights(1, 2)
-    accumulate(a2, w2, 3, inner)
+
+    @pl.when(even)
+    def _():
+        accumulate(a1, w1, 0, inner)
+        send(1, 1, "x_middle")
+        second(0, inner)
+        accumulate(a2, w2, 3, inner)
+        hear(0, 0, *halos)
+        accumulate(a1, w1, 0, outer)
+        second(0, outer)
+        send(1, 0, *sides, *edges, "x_middle")
+
+    @pl.when(jnp.logical_not(even))
+    def _():
+        begun.discard((True, 1, inner))
+        hear(0, 0, *halos)
+        accumulate(a1, w1, 0, outer)
+        send(1, 1, "x_middle")
+        second(0, outer)
+        send(1, 0, *sides, *edges)
+        accumulate(a1, w1, 0, inner)
+        second(0, inner)
+        accumulate(a2, w2, 3, inner)
+        send(1, 0, "x_middle")
+
     hear(1, 1, *sides)
     send(1, 1, *halos)
     hear(1, 1, *edges)
@@ -239,14 +274,14 @@
     need_weights(1, 1)
     accumulate(a2, w2, 2, inner)
     accumulate(a2, w2, 3, outer)
-    hear(1, 0, *sides)
-    send(1, 0, *halos)
-    hear(1, 0, *edges)
-    send(1, 0, *forwards)
-    accumulate(a2, w2, 2, outer)
     hear(1, 1, "x_middle")
     need_weights(1, 0)
     accumulate(a2, w2, 1, inner)
+    hear(1, 0, *sides)
+    send(1, 0, *halos)
+    accumulate(a2, w2, 2, outer)
+    hear(1, 0, *edges)
+    send(1, 0, *forwards)
     hear(1, 1, *halos)
     decoded(1, inner)
     accumulate(a2, w2, 1, outer)
@@ -294,11 +329,11 @@
             vmem((width,), jnp.float32),
             vmem(halo, jnp.bfloat16),
             vmem(halo, jnp.bfloat16),
-            vmem((taps, 3 * taps), jnp.bfloat16),
-            vmem((taps, 3 * taps), jnp.bfloat16),
+            vmem((3, width, 3 * taps), jnp.bfloat16),
+            vmem((3, width, 3 * taps), jnp.bfloat16),
             vmem((nframe, nrow, ncol, taps), jnp.float32),
             pltpu.SemaphoreType.DMA((3,)),
-            pltpu.SemaphoreType.DMA((2, 3, 3, 3)),
+            pltpu.SemaphoreType.DMA((2, 3, 3)),
             pltpu.SemaphoreType.DMA((2, 2, 9)),
             pltpu.SemaphoreType.DMA((2, 2, 7)),
         ],

time: 37.6 us -> 36.1 us (0.960); the launches traced: 37 us -> 35.9 us
  Pallas kernels: 34.1 us -> 33 us
    pallas_call x1, Pallas kernels: 34.1 us -> 33 us  [shards(): pl.pallas_call(kernel, out_shape=jax.ShapeDtypeStruct(frames.shape, frame...]
where the time goes in v3:
time: 36.1 us; the launch traced here: 35.9 us
  Pallas kernels  33 us (91%)
  local copies, waits for them, and re-layouts  2.24 us (6%)
  between operations  0.67 us (2%)
    pallas_call x1, Pallas kernels, shards(): pl.pallas_call(kernel, out_shape=jax.ShapeDtypeStruct(frames.shape, frame...  33 us
    unnamed x5, local copies, waits for them, and re-layouts  2.24 us

profile of v3, /device:TPU:6, one launch (start us, length us, event | category | flops | bytes accessed | tf_op | source)
XLA Modules:
  0.0 35.9 jit_solution(9354993764020949676)
XLA Ops:
  0.7 0.0 copy-start
  0.7 0.7 %copy-done = f32[384]{0:T(512)S(1)} copy-done((f32[384]{0:T(512)S(1)}, f32[384]{0:T(512)}, u32[]{:S(2)}) %copy-start) | copy-done | bytes 1560
  1.3 0.0 copy-start.1
  1.3 0.7 %copy-done.1 = f32[384]{0:T(512)S(1)} copy-done((f32[384]{0:T(512)S(1)}, f32[384]{0:T(512)}, u32[]{:S(2)}) %copy-start.1) | copy-done | bytes 1560
  2.0 33.0 %shard_map.64 = bf16[2,4,128,384]{3,2,1,0:T(8,128)(2,1)S(1)} custom-call(s32[1]{0:T(128)S(6)} %copy.8.refs_0_, bf16[2,4,128,384]{3,2,1,0:T(8,128)(2,1)} %refs_1_.1, f32[384]{0:T(512)S(1)} %copy-done, f32[384]{0:T(512)S(1)} %copy-done.1, bf16[3,3,3,384,384]{4,3,2,1,0:T(8,128)(2,1)} %refs_4_.1, bf16[3,3,3,384,384]{4,3,2,1,0:T(8,128)(2,1)} %refs_5_.1), custom_call_target="tpu_custom_call" | custom-call | tf_op jit(solution)/shard_map/pallas_call | solution.py:314
  35.0 0.9 %copy.9 = bf16[2,4,128,384]{3,2,1,0:T(8,128)(2,1)} copy(bf16[2,4,128,384]{3,2,1,0:T(8,128)(2,1)S(1)} %shard_map.64) | data formatting | bytes 1572864
Async XLA Ops:
  0.7 0.7 %copy-start = (f32[384]{0:T(512)S(1)}, f32[384]{0:T(512)}, u32[]{:S(2)}) copy-start(f32[384]{0:T(512)} %refs_2_.1) | copy-start | bytes 4612
  1.3 0.7 %copy-start.1 = (f32[384]{0:T(512)S(1)}, f32[384]{0:T(512)}, u32[]{:S(2)}) copy-start(f32[384]{0:T(512)} %refs_3_.1) | copy-start | bytes 4612

commit v4 on v3

--- a/solution.py
+++ b/solution.py
@@ -277,20 +277,28 @@
     hear(1, 1, "x_middle")
     need_weights(1, 0)
     accumulate(a2, w2, 1, inner)
+    begun.update({(True, 0, outer), (True, 1, outer)})
+    started.difference_update({(0, 0), (0, 3)})
+    partly(a2, w2, 2, 0, (1, 2))
+    partly(a2, w2, 2, 3, (0, 1))
     hear(1, 0, *sides)
     send(1, 0, *halos)
-    accumulate(a2, w2, 2, outer)
     hear(1, 0, *edges)
     send(1, 0, *forwards)
+    partly(a2, w2, 2, 0, (0,))
+    partly(a2, w2, 2, 3, (2,))
     hear(1, 1, *halos)
     decoded(1, inner)
     accumulate(a2, w2, 1, outer)
     hear(1, 0, "x_middle")
     decoded(1, outer)
     accumulate(a2, w2, 0, inner)
+    partly(a2, w2, 0, 0, (1, 2))
+    partly(a2, w2, 0, 3, (0, 1))
+    decoded(0, inner)
     hear(1, 0, *halos)
-    decoded(0, inner)
-    accumulate(a2, w2, 0, outer)
+    partly(a2, w2, 0, 0, (0,))
+    partly(a2, w2, 0, 3, (2,))
     decoded(0, outer)
 
     for k in (0, 1):

time: 36.1 us -> 35.3 us (0.978)
  Pallas kernels: 33 us -> 32.2 us
    pallas_call x1, Pallas kernels: 33 us -> 32.2 us  [shards(): pl.pallas_call(kernel, out_shape=jax.ShapeDtypeStruct(frames.shape, frame...]
where the time goes in v4:
time: 35.3 us; the launch traced here: 35.1 us
  Pallas kernels  32.2 us (91%)
  local copies, waits for them, and re-layouts  2.24 us (6%)
  between operations  0.67 us (2%)
    pallas_call x1, Pallas kernels, shards(): pl.pallas_call(kernel, out_shape=jax.ShapeDtypeStruct(frames.shape, frame...  32.2 us
    unnamed x5, local copies, waits for them, and re-layouts  2.24 us

profile of v4, /device:TPU:6, one launch (start us, length us, event | category | flops | bytes accessed | tf_op | source)
XLA Modules:
  0.0 35.1 jit_solution(2103259239309359691)
XLA Ops:
  0.7 0.0 copy-start
  0.7 0.7 %copy-done = f32[384]{0:T(512)S(1)} copy-done((f32[384]{0:T(512)S(1)}, f32[384]{0:T(512)}, u32[]{:S(2)}) %copy-start) | copy-done | bytes 1560
  1.3 0.0 copy-start.1
  1.3 0.7 %copy-done.1 = f32[384]{0:T(512)S(1)} copy-done((f32[384]{0:T(512)S(1)}, f32[384]{0:T(512)}, u32[]{:S(2)}) %copy-start.1) | copy-done | bytes 1560
  2.0 32.2 %shard_map.64 = bf16[2,4,128,384]{3,2,1,0:T(8,128)(2,1)S(1)} custom-call(s32[1]{0:T(128)S(6)} %copy.8.refs_0_, bf16[2,4,128,384]{3,2,1,0:T(8,128)(2,1)} %refs_1_.1, f32[384]{0:T(512)S(1)} %copy-done, f32[384]{0:T(512)S(1)} %copy-done.1, bf16[3,3,3,384,384]{4,3,2,1,0:T(8,128)(2,1)} %refs_4_.1, bf16[3,3,3,384,384]{4,3,2,1,0:T(8,128)(2,1)} %refs_5_.1), custom_call_target="tpu_custom_call" | custom-call | tf_op jit(solution)/shard_map/pallas_call | solution.py:322
  34.3 0.9 %copy.9 = bf16[2,4,128,384]{3,2,1,0:T(8,128)(2,1)} copy(bf16[2,4,128,384]{3,2,1,0:T(8,128)(2,1)S(1)} %shard_map.64) | data formatting | bytes 1572864
Async XLA Ops:
  0.7 0.7 %copy-start = (f32[384]{0:T(512)S(1)}, f32[384]{0:T(512)}, u32[]{:S(2)}) copy-start(f32[384]{0:T(512)} %refs_2_.1) | copy-start | bytes 4612
  1.3 0.7 %copy-start.1 = (f32[384]{0:T(512)S(1)}, f32[384]{0:T(512)}, u32[]{:S(2)}) copy-start(f32[384]{0:T(512)} %refs_3_.1) | copy-start | bytes 4612

commit v5 on v4

--- a/solution.py
+++ b/solution.py
@@ -296,17 +296,16 @@
     partly(a2, w2, 0, 0, (1, 2))
     partly(a2, w2, 0, 3, (0, 1))
     decoded(0, inner)
-    hear(1, 0, *halos)
-    partly(a2, w2, 0, 0, (0,))
-    partly(a2, w2, 0, 3, (2,))
-    decoded(0, outer)
-
     for k in (0, 1):
         for f in (0, 1):
             for kind in may_send:
                 @pl.when(may_send[kind])
                 def _():
                     route(k, f, kind).wait_send()
+    hear(1, 0, *halos)
+    partly(a2, w2, 0, 0, (0,))
+    partly(a2, w2, 0, 3, (2,))
+    decoded(0, outer)
 
 
 def shards(frames, live_rows, gain_first, conv_first, gain_second, conv_second):

time: 35.3 us -> 35.3 us (level)
  no operation moved by 1% of the time
where the time goes in v5:
time: 35.3 us; the launch traced here: 35.1 us
  Pallas kernels  32.2 us (91%)
  local copies, waits for them, and re-layouts  2.24 us (6%)
  between operations  0.67 us (2%)
    pallas_call x1, Pallas kernels, shards(): pl.pallas_call(kernel, out_shape=jax.ShapeDtypeStruct(frames.shape, frame...  32.2 us
    unnamed x5, local copies, waits for them, and re-layouts  2.24 us

profile of v5, /device:TPU:6, one launch (start us, length us, event | category | flops | bytes accessed | tf_op | source)
XLA Modules:
  0.0 35.1 jit_solution(7244261251487801)
XLA Ops:
  0.7 0.0 copy-start
  0.7 0.7 %copy-done = f32[384]{0:T(512)S(1)} copy-done((f32[384]{0:T(512)S(1)}, f32[384]{0:T(512)}, u32[]{:S(2)}) %copy-start) | copy-done | bytes 1560
  1.3 0.0 copy-start.1
  1.3 0.7 %copy-done.1 = f32[384]{0:T(512)S(1)} copy-done((f32[384]{0:T(512)S(1)}, f32[384]{0:T(512)}, u32[]{:S(2)}) %copy-start.1) | copy-done | bytes 1560
  2.0 32.2 %shard_map.64 = bf16[2,4,128,384]{3,2,1,0:T(8,128)(2,1)S(1)} custom-call(s32[1]{0:T(128)S(6)} %copy.8.refs_0_, bf16[2,4,128,384]{3,2,1,0:T(8,128)(2,1)} %refs_1_.1, f32[384]{0:T(512)S(1)} %copy-done, f32[384]{0:T(512)S(1)} %copy-done.1, bf16[3,3,3,384,384]{4,3,2,1,0:T(8,128)(2,1)} %refs_4_.1, bf16[3,3,3,384,384]{4,3,2,1,0:T(8,128)(2,1)} %refs_5_.1), custom_call_target="tpu_custom_call" | custom-call | tf_op jit(solution)/shard_map/pallas_call | solution.py:321
  34.2 0.9 %copy.9 = bf16[2,4,128,384]{3,2,1,0:T(8,128)(2,1)} copy(bf16[2,4,128,384]{3,2,1,0:T(8,128)(2,1)S(1)} %shard_map.64) | data formatting | bytes 1572864
Async XLA Ops:
  0.7 0.7 %copy-start = (f32[384]{0:T(512)S(1)}, f32[384]{0:T(512)}, u32[]{:S(2)}) copy-start(f32[384]{0:T(512)} %refs_2_.1) | copy-start | bytes 4612
  1.3 0.7 %copy-start.1 = (f32[384]{0:T(512)S(1)}, f32[384]{0:T(512)}, u32[]{:S(2)}) copy-start(f32[384]{0:T(512)} %refs_3_.1) | copy-start | bytes 4612
